TPU v7x, 128 devices: a whole 4x4x4 slice. The times are simulated.
128 devices in a mesh: cls: 8 (over y, core), mem: 16 (over z, x).
Axes of the slice: x: 4, y: 4, z: 4, core: 2. Of those that a mesh axis runs over, the one named last changes fastest.
Arguments:
- images: bfloat16 [3072, 65536], P(('cls', 'mem')), may hold values from -6 to 6
- owner_group: int32 [3072, 1], P(('cls', 'mem')), may hold values from 0 to 7; in each aligned block of 24 rows (0 to 23, 24 to 47, ...) at most 6 rows name the same one
- bin_in_group: int32 [3072], P(('cls', 'mem')), may hold values from 0 to 7
- defocus: bfloat16 [3072], P(('cls', 'mem')), may hold values from 0.5 to 2
- projections: bfloat16 [64, 65536], P('cls'), may hold values from -6 to 6
- sketch_weight: bfloat16 [64, 48], replicated, may hold values from -0.875 to 0.875
Outputs:
- basis: bfloat16 [8, 64, 65536], P('cls', None, 'mem')
Inputs may be any that keep to these rules, and one draw needn't show every extreme that they name: `owner_group`: in the particles of one device no class group is named more than 6 times, and 6 is reached on some device.
All inputs are finite; a program needn't handle non-finite values.
Results may differ from a plain program's by a relative error of at most 0.012.
The roundings to bfloat16 on the way count: a program that leaves them out, or rounds other values in their place, can miss the bound.
Values may be sent and summed in bfloat16 or wider, within the bound.
A program may use at most 128 MiB of HBM per device.

v0:
```python
import math
import jax
import jax.numpy as jnp
from jax import lax
from jax.sharding import PartitionSpec as P

SIDE = 256
CAP = 6
HI = lax.Precision.HIGHEST


def wave_slice(first, width):
    position = first + jnp.arange(width, dtype=jnp.int32)
    column = position % SIDE
    row_idx = position // SIDE
    fx = jnp.where(column < SIDE // 2, column, column - SIDE).astype(jnp.float32) / SIDE
    fy = jnp.where(row_idx < SIDE // 2, row_idx, row_idx - SIDE).astype(jnp.float32) / SIDE
    return 160.0 * (fx * fx + fy * fy)


def bmm(a, b):
    return jnp.einsum("nij,njk->nik", a, b, precision=HI)


def coefficients(gram, pixels):
    total = jnp.trace(gram, axis1=1, axis2=2)[:, None, None] + 1e-06
    scaled = gram / total
    ident = jnp.eye(gram.shape[1], dtype=jnp.float32)[None]
    first = 1.5 * ident - 0.5 * scaled
    later = bmm(bmm(first, scaled), first)
    second = 1.5 * ident - 0.5 * later
    return bmm(second, first) * jnp.sqrt(pixels / total)


def tree(gram, n_mem, rank, pixels):
    blocks = n_mem
    k = gram.reshape(n_mem, rank, n_mem, rank)
    chain = None
    while True:
        diag = jnp.stack([k[i, :, i, :] for i in range(blocks)])
        c = coefficients(diag, pixels)
        if chain is None:
            chain = c[:, :, None, :]
        else:
            chain = jnp.einsum("nij,njmk->nimk", c, chain, precision=HI)
        if blocks == 1:
            return chain.reshape(rank, n_mem * rank)
        k = jnp.einsum("aij,ajbk->aibk", c, k, precision=HI)
        k = jnp.einsum("aibk,blk->aibl", k, c, precision=HI)
        half = blocks // 2
        k = k.reshape(half, 2, rank, half, 2, rank).sum(axis=(1, 4))
        chain = (
            chain.reshape(half, 2, rank, -1, rank)
            .transpose(0, 2, 1, 3, 4)
            .reshape(half, rank, -1, rank)
        )
        blocks = half


def body(images, owner_group, bin_in_group, defocus, projections, sketch_weight):
    n_cls = lax.axis_size("cls")
    n_mem = lax.axis_size("mem")
    pixels = images.shape[1]
    width = pixels // n_mem
    member = lax.axis_index("mem")
    cls = lax.axis_index("cls")
    p_dev = images.shape[0]
    bins_here = projections.shape[0]
    rank_k = sketch_weight.shape[0]
    owners = owner_group[:, 0]
    onehot = (owners[:, None] == jnp.arange(n_cls, dtype=jnp.int32)[None, :]).astype(jnp.int32)
    before = jnp.cumsum(onehot, axis=0) - onehot
    rank = jnp.sum(onehot * before, axis=1)
    target = owners * CAP + rank
    meta = jnp.stack(
        [target.astype(jnp.float32), defocus.astype(jnp.float32), bin_in_group.astype(jnp.float32)]
    )
    meta = lax.all_gather(meta, ("cls", "mem"), tiled=False).reshape(n_cls, n_mem, 3, p_dev)
    rows = lax.all_to_all(images, "mem", split_axis=1, concat_axis=0, tiled=True)
    rows = rows.reshape(n_mem, p_dev, width)
    mine = lax.dynamic_index_in_dim(meta, cls, 0, keepdims=False)[:, 0]
    select = jnp.arange(n_cls * CAP, dtype=jnp.float32)[None, :, None] == mine[:, None, :]
    sent = jnp.einsum(
        "mti,mip->mtp", select.astype(jnp.bfloat16), rows, preferred_element_type=jnp.float32
    ).astype(jnp.bfloat16)
    sent = (
        sent.reshape(n_mem, n_cls, CAP, width)
        .transpose(1, 0, 2, 3)
        .reshape(n_cls * n_mem * CAP, width)
    )
    got = lax.all_to_all(sent, "cls", split_axis=0, concat_axis=0, tiled=True)
    slot = (cls * CAP + jnp.arange(CAP, dtype=jnp.int32)).astype(jnp.float32)
    pick = (slot[None, None, :, None] == meta[:, :, None, 0, :]).astype(jnp.float32)
    focus = jnp.sum(pick * meta[:, :, None, 1, :], axis=-1).reshape(-1)
    local_bin = jnp.sum(pick * meta[:, :, None, 2, :], axis=-1)
    valid = jnp.sum(pick, axis=-1)
    bins = jnp.arange(bins_here, dtype=jnp.float32)
    table = jnp.where((local_bin[..., None] == bins) & (valid[..., None] > 0.5), 1.0, 0.0)
    table = table.reshape(-1, bins_here).astype(jnp.bfloat16)
    proj = lax.dynamic_slice_in_dim(projections, member * width, width, 1)
    chosen = jnp.dot(table, proj, preferred_element_type=jnp.float32)
    chi = focus[:, None] * wave_slice(member * width, width)[None, :]
    ctf = -math.sqrt(1.01) * jnp.sin(chi + math.atan(0.1))
    residual = (got.astype(jnp.float32) - ctf * chosen).astype(jnp.bfloat16)
    residual = (
        residual.reshape(n_cls, n_mem, CAP, width)
        .transpose(1, 0, 2, 3)
        .reshape(n_mem, n_cls * CAP, width)
    )
    sketch = jnp.einsum(
        "ks,msp->mkp", sketch_weight, residual, preferred_element_type=jnp.float32
    ).astype(jnp.bfloat16)
    sketch = sketch.reshape(n_mem * rank_k, width)
    gram = jnp.einsum("ap,bp->ab", sketch, sketch, preferred_element_type=jnp.float32)
    gram = lax.psum(gram, "mem")
    coef = tree(gram, n_mem, rank_k, float(pixels)).astype(jnp.bfloat16)
    result = jnp.dot(coef, sketch, preferred_element_type=jnp.float32).astype(jnp.bfloat16)
    return result[None]


def solution(mesh):
    in_specs = (
        P(("cls", "mem"), None),
        P(("cls", "mem"), None),
        P(("cls", "mem")),
        P(("cls", "mem")),
        P("cls", None),
        P(),
    )
    out_specs = P("cls", None, "mem")
    return jax.shard_map(body, mesh=mesh, in_specs=in_specs, out_specs=out_specs, check_vma=False)
```

profile of v0, /device:TPU:1, one launch (start us, length us, event | category | flops | bytes accessed | tf_op | source)
XLA Modules:
  0.0 546.3 jit_solution(17044176956349966713)
XLA Ops:
  6.5 4.0 copy.191
  10.6 8.5 %all-to-all-start = ((bf16[24,16,4096]{2,0,1:T(8,128)(2,1)}), bf16[24,16,4096]{2,0,1:T(8,128)(2,1)}, u32[]{:S(2)}, u32[]{:S(2)}) async-start(bf16[24,16,4096]{2,0,1:T(8,128)(2,1)} %bitcast.266), calls=%async_computation | async-start | bytes 6291456 | tf_op jit(solution)/shard_map/all_to_all | solution.py:79
  19.4 96.3 %all-gather.1 = f32[128,3,24]{2,1,0:T(4,128)S(1)} all-gather(f32[1,3,24]{2,1,0:T(4,128)S(1)} %maximum_bitcast_fusion), channel_id=2, replica_groups=mesh['cls'=8,'mem'=16] {'cls','mem'}, dimensions={0}, use_global_device_ids=true | all-gather | bytes 37152 | tf_op jit(solution)/shard_map/all_gather | solution.py:78
  115.8 3.8 convolution_convert_fusion.1
  119.6 3.4 copy.115
  123.1 3.4 copy.116
  126.5 6.3 %copy.117 = bf16[8,96,4096]{2,1,0:T(8,128)(2,1)} copy(bf16[8,96,4096]{2,0,1:T(8,128)(2,1)S(1)} %bitcast.264) | data formatting | bytes 12582912 | tf_op jit(solution)/shard_map/all_to_all | solution.py:91
  132.8 5.8 %all-to-all-start.1 = ((bf16[8,96,4096]{2,1,0:T(8,128)(2,1)}), bf16[8,96,4096]{2,1,0:T(8,128)(2,1)}, u32[]{:S(2)}, u32[]{:S(2)}) async-start(bf16[8,96,4096]{2,1,0:T(8,128)(2,1)} %copy.117), calls=%async_computation.1 | async-start | bytes 12582912 | tf_op jit(solution)/shard_map/all_to_all | solution.py:91
  140.1 69.9 %all-to-all-done.1 = bf16[8,96,4096]{2,1,0:T(8,128)(2,1)} async-done(((bf16[8,96,4096]{2,1,0:T(8,128)(2,1)}), bf16[8,96,4096]{2,1,0:T(8,128)(2,1)}, u32[]{:S(2)}, u32[]{:S(2)}) %all-to-all-start.1) | async-done | bytes 6291488 | tf_op jit(solution)/shard_map/all_to_all | solution.py:91
  210.0 47.5 %fusion = bf16[768,4096]{1,0:T(8,128)(2,1)} fusion(bf16[768,4096]{1,0:T(8,128)(2,1)} %bitcast.88, f32[4096]{0:T(1024)S(1)} %fusion.85, f32[768]{0:T(1024)S(1)} %mul.219, f32[768]{0:T(1024)S(1)} %eq.134, pred[768]{0:T(1024)(128)(4,1)S(1)} %gt.16, bf16[8,65536]{1,0:T(8,128)(2,1)S(1)} %copy-done, s32[]{:T(128)S(6)} %select_n.80), kind=kOutput, calls=%fused_computation.1 | convolution fusion | flops 72376320 | bytes 12674052 | tf_op jit(solution)/shard_map/dot_general | solution.py:101
  257.5 10.1 %reshape.271 = bf16[8,16,6,4096]{3,2,1,0:T(8,128)(2,1)} reshape(bf16[768,4096]{1,0:T(8,128)(2,1)} %fusion) | data formatting | bytes 12582912 | tf_op jit(solution)/shard_map/reshape | solution.py:106
  267.7 7.0 %copy.125 = bf16[16,8,6,4096]{3,0,2,1:T(8,128)(2,1)S(1)} copy(bf16[16,8,6,4096]{3,2,0,1:T(8,128)(2,1)} %bitcast.261) | data formatting | bytes 12582912 | tf_op jit(solution)/shard_map/transpose | solution.py:107
  274.6 5.7 %convolution_convert_fusion = bf16[16,4096,64]{1,2,0:T(8,128)(2,1)S(1)} fusion(bf16[16,48,4096]{2,0,1:T(8,128)(2,1)S(1)} %bitcast.265, bf16[64,48]{0,1:T(8,128)(2,1)S(1)} %copy-done.4), kind=kOutput, calls=%fused_computation.4 | convolution fusion | flops 406847488 | bytes 14686208 | tf_op jit(solution)/shard_map/ks,msp->mkp/dot_general | solution.py:110
  280.3 3.2 copy-done.2
  283.5 10.8 %fusion.140 = f32[1024,1024]{1,0:T(8,128)} fusion(bf16[1024,4096]{1,0:T(8,128)(2,1)S(1)} %bitcast.259), kind=kOutput, calls=%fused_computation.242 | convolution fusion | flops 8589934592 | bytes 12582912 | tf_op jit(solution)/shard_map/ap,bp->ab/dot_general | solution.py:114
  294.3 7.3 %reshape.274 = f32[16,64,16,64]{3,2,1,0:T(8,128)} reshape(f32[1024,1024]{1,0:T(8,128)} %fusion.140) | data formatting | bytes 8388608 | tf_op jit(solution)/shard_map/reshape | solution.py:37
  301.6 9.2 %copy.127 = f32[16,64,16,64]{3,1,2,0:T(8,128)} copy(f32[16,64,16,64]{3,2,1,0:T(8,128)} %reshape.274) | data formatting | bytes 8388608 | tf_op jit(solution)/shard_map/reshape | solution.py:37
  310.9 139.2 %all-reduce.2.cloned.1.call-done = f32[16,64,16,64]{3,1,2,0:T(8,128)} async-done(((f32[16,64,16,64]{3,1,2,0:T(8,128)}), f32[16,64,16,64]{3,1,2,0:T(8,128)}) %all-reduce.2.cloned.1.call-update) | async-done | bytes 4194320 | tf_op jit(solution)/shard_map/psum | solution.py:115
  450.1 0.9 constant_dynamic-update-slice_fusion.15
  451.0 0.9 constant_dynamic-update-slice_fusion.14
  451.9 1.1 constant_dynamic-update-slice_fusion.13
  463.1 0.8 fusion.19
  465.3 8.7 %fusion.1 = f32[16,64,16,64]{3,1,0,2:T(8,128)S(1)} fusion(f32[16,64,16,64]{3,1,2,0:T(8,128)S(1)} %copy-done.3, f32[16,64,64]{2,1,0:T(8,128)S(1)} %convolution_multiply_fusion), kind=kOutput, calls=%fused_computation.2 | convolution fusion | flops 805306368 | bytes 8650752 | tf_op jit(solution)/shard_map/aij,ajbk->aibk/dot_general | solution.py:48
  474.0 26.4 %fusion.16 = f32[16,64,16,64]{3,1,2,0:T(8,128)} fusion(f32[16,64,16,64]{3,1,0,2:T(8,128)S(1)} %fusion.1, f32[16,64,64]{2,1,0:T(8,128)S(1)} %convolution_multiply_fusion), kind=kOutput, calls=%fused_computation.36 | convolution fusion | flops 805306368 | bytes 8650752 | tf_op jit(solution)/shard_map/aibk,blk->aibl/dot_general | solution.py:49
  500.4 4.6 reduce_sum.131
  507.4 6.1 %fusion.28 = f32[8,64,8,64]{3,1,0,2:T(8,128)S(1)} fusion(f32[8,64,8,64]{1,3,0,2:T(8,128)S(1)} %reduce_sum.131, f32[8,64,64]{2,1,0:T(8,128)S(1)} %convolution_multiply_fusion.2), kind=kOutput, calls=%fused_computation.53 | convolution fusion | flops 201326592 | bytes 2228224 | tf_op jit(solution)/shard_map/aij,ajbk->aibk/dot_general | solution.py:48
  513.5 1.4 fusion.24
  514.8 6.0 %fusion.26 = f32[8,64,8,64]{3,1,2,0:T(8,128)S(1)} fusion(f32[8,64,8,64]{3,1,0,2:T(8,128)S(1)} %fusion.28, f32[8,64,64]{2,1,0:T(8,128)S(1)} %convolution_multiply_fusion.2), kind=kOutput, calls=%fused_computation.51 | convolution fusion | flops 201326592 | bytes 2228224 | tf_op jit(solution)/shard_map/aibk,blk->aibl/dot_general | solution.py:49
  522.7 1.6 fusion.46
  524.3 1.9 fusion.14
  526.2 1.6 fusion.42
  533.3 5.7 %fusion.4 = bf16[1,64,4096]{2,1,0:T(8,128)(2,1)} fusion(bf16[64,1024]{1,0:T(8,128)(2,1)S(1)} %convolution_convert_fusion.3, bf16[1024,4096]{1,0:T(8,128)(2,1)} %bitcast.260), kind=kOutput, calls=%fused_computation.8 | convolution fusion | flops 537133056 | bytes 9043968 | tf_op jit(solution)/shard_map/dot_general | solution.py:117
  (111 shorter events, 22.0 us)
Async XLA Ops:
  6.5 203.5 %copy-start = (bf16[8,65536]{1,0:T(8,128)(2,1)S(1)}, bf16[8,65536]{1,0:T(8,128)(2,1)}, u32[]{:S(2)}) copy-start(bf16[8,65536]{1,0:T(8,128)(2,1)} %param.10) | copy-start | bytes 3145732
  6.5 12.5 %copy-start.5 = (s32[24,1]{0,1:T(1,128)S(1)}, s32[24,1]{0,1:T(1,128)}, u32[]{:S(2)}) copy-start(s32[24,1]{0,1:T(1,128)} %param.7) | copy-start | bytes 292
  6.5 12.8 %copy-start.6 = (s32[24]{0:T(128)S(1)}, s32[24]{0:T(128)}, u32[]{:S(2)}) copy-start(s32[24]{0:T(128)} %param.8) | copy-start | bytes 292
  6.5 12.9 %copy-start.7 = (bf16[24]{0:T(256)(128)(2,1)S(1)}, bf16[24]{0:T(256)(128)(2,1)}, u32[]{:S(2)}) copy-start(bf16[24]{0:T(256)(128)(2,1)} %param.9) | copy-start | bytes 148
  10.6 105.2 %all-to-all-start = ((bf16[24,16,4096]{2,0,1:T(8,128)(2,1)}), bf16[24,16,4096]{2,0,1:T(8,128)(2,1)}, u32[]{:S(2)}, u32[]{:S(2)}) async-start(bf16[24,16,4096]{2,0,1:T(8,128)(2,1)} %bitcast.266), calls=%async_computation | async-start | bytes 6291456 | tf_op jit(solution)/shard_map/all_to_all | solution.py:79
  132.8 77.2 %all-to-all-start.1 = ((bf16[8,96,4096]{2,1,0:T(8,128)(2,1)}), bf16[8,96,4096]{2,1,0:T(8,128)(2,1)}, u32[]{:S(2)}, u32[]{:S(2)}) async-start(bf16[8,96,4096]{2,1,0:T(8,128)(2,1)} %copy.117), calls=%async_computation.1 | async-start | bytes 12582912 | tf_op jit(solution)/shard_map/all_to_all | solution.py:91
  138.6 311.4 %all-reduce.2.cloned.1.call-start = ((), (), s32[]{:S(2)}) async-start(), calls=%async_computation.2 | async-start | bytes 16777216 | tf_op jit(solution)/shard_map/psum | solution.py:115
  267.6 7.0 %copy-start.4 = (bf16[64,48]{0,1:T(8,128)(2,1)S(1)}, bf16[64,48]{0,1:T(8,128)(2,1)}, u32[]{:S(2)}) copy-start(bf16[64,48]{0,1:T(8,128)(2,1)} %param.11) | copy-start | bytes 18436
  280.3 3.2 copy-start.2
  450.1 15.3 %copy-start.3 = (f32[16,64,16,64]{3,1,2,0:T(8,128)S(1)}, f32[16,64,16,64]{3,1,2,0:T(8,128)}, u32[]{:S(2)}) copy-start(f32[16,64,16,64]{3,1,2,0:T(8,128)} %all-reduce.2.cloned.1.call-done) | copy-start | bytes 12582916
  530.4 8.6 %copy-start.1 = (bf16[8,65536]{1,0:T(8,128)(2,1)S(1)}, bf16[8,65536]{1,0:T(8,128)(2,1)}, u32[]{:S(2)}) copy-start(bf16[8,65536]{1,0:T(8,128)(2,1)} %param.10) | copy-start | bytes 3145732
Sparse Core Ops, SparseCore 0:
  310.9 139.0 all-reduce.1
where the time goes:
time: 557 us; the launch traced here: 546 us
  waiting for transfers between devices  209 us (38%)
  matrix products  135 us (24%)
  blocking collectives  96.3 us (17%)
  local copies, waits for them, and re-layouts  69.5 us (12%)
  between operations  15.1 us (3%)
  starting transfers between devices  14.3 us (3%)
  other arithmetic  7.06 us (1%)
    psum x1, waiting for transfers between devices, body(): gram = lax.psum(gram, 'mem')  139 us
    all_gather x1, blocking collectives, body(): lax.all_gather(meta, ('cls', 'mem'), tiled=False)  96.3 us
    all_to_all x1, waiting for transfers between devices, body(): got = lax.all_to_all(sent, 'cls', split_axis=0, concat_axis=0, tiled=True)  69.9 us
    dot_general x1, matrix products, body(): chosen = jnp.dot(table, proj, preferred_element_type=jnp.float32)  47.5 us
    dot_general x4, matrix products, tree(): k = jnp.einsum('aibk,blk->aibl', k, c, precision=HI)  34.3 us
    dot_general x4, matrix products, tree(): k = jnp.einsum('aij,ajbk->aibk', c, k, precision=HI)  16.8 us
    reshape x2, local copies, waits for them, and re-layouts, tree(): k = gram.reshape(n_mem, rank, n_mem, rank)  16.5 us
    unnamed x52, local copies, waits for them, and re-layouts  16.4 us
  transfers between devices with their start and end apart: 3, of which 2 were waited for; matrix products, arithmetic and copies ran while one was open for 0% of the time, Pallas kernels for 0%

commit v1 on v0

--- a/solution.py
+++ b/solution.py
@@ -7,6 +7,28 @@
 SIDE = 256
 CAP = 6
 HI = lax.Precision.HIGHEST
+
+
+def split_up(shard, dim, devices):
+    before, after = (shard.shape[:dim], shard.shape[dim + 1 :])
+    return jnp.moveaxis(shard.reshape(*before, devices, -1, *after), dim, 0)
+
+
+def joined_along(parts, dim):
+    parts = jnp.moveaxis(parts, 0, dim)
+    shape = parts.shape
+    return parts.reshape(*shape[:dim], shape[dim] * shape[dim + 1], *shape[dim + 2 :])
+
+
+def pairwise_exchange(array, axis, split_dim, concat_dim):
+    size, position = (lax.axis_size(axis), lax.axis_index(axis))
+    tiles = split_up(array, split_dim, size)
+    gathered = [tiles[position]]
+    for step in range(1, size):
+        sent = tiles[position ^ step]
+        gathered.append(lax.ppermute(sent, axis, [(i, i ^ step) for i in range(size)]))
+    tiles = jnp.stack(gathered)[position ^ jnp.arange(size)]
+    return joined_along(tiles, concat_dim)
 
 
 def wave_slice(first, width):
@@ -88,7 +110,7 @@
         .transpose(1, 0, 2, 3)
         .reshape(n_cls * n_mem * CAP, width)
     )
-    got = lax.all_to_all(sent, "cls", split_axis=0, concat_axis=0, tiled=True)
+    got = pairwise_exchange(sent, "cls", 0, 0)
     slot = (cls * CAP + jnp.arange(CAP, dtype=jnp.int32)).astype(jnp.float32)
     pick = (slot[None, None, :, None] == meta[:, :, None, 0, :]).astype(jnp.float32)
     focus = jnp.sum(pick * meta[:, :, None, 1, :], axis=-1).reshape(-1)

time: 557 us -> 596 us (1.070)
  local copies, waits for them, and re-layouts: 69.5 us -> 105 us
  waiting for transfers between devices: 209 us -> 200 us
  matrix products: 135 us -> 142 us
  starting transfers between devices: 14.3 us -> 20.6 us
    all_to_all x1 -> x0, waiting for transfers between devices: 69.9 us -> none  [body(): got = lax.all_to_all(sent, 'cls', split_axis=0, concat_axis=0, tiled=True)]
    ppermute x0 -> x7, waiting for transfers between devices: none -> 59.4 us  [pairwise_exchange(): lax.ppermute(sent, axis, [(i, i ^ step) for i in range(size)])]
    unnamed x52 -> x76, local copies, waits for them, and re-layouts: 16.4 us -> 34.6 us
    dynamic_slice x0 -> x1, local copies, waits for them, and re-layouts: none -> 16.1 us  [pairwise_exchange(): sent = tiles[position ^ step]]
    ppermute x0 -> x7, starting transfers between devices: none -> 12.1 us  [pairwise_exchange(): lax.ppermute(sent, axis, [(i, i ^ step) for i in range(size)])]
    dot_general x1, matrix products: 47.5 us -> 56 us  [body(): chosen = jnp.dot(table, proj, preferred_element_type=jnp.float32)]
    gather x0 -> x1, local copies, waits for them, and re-layouts: none -> 6.39 us  [pairwise_exchange(): tiles = jnp.stack(gathered)[position ^ jnp.arange(size)]]
    all_to_all x1 -> x0, local copies, waits for them, and re-layouts: 6.28 us -> none  [body(): got = lax.all_to_all(sent, 'cls', split_axis=0, concat_axis=0, tiled=True)]
  transfers between devices with their start and end apart: 3 -> 9, of which waited for: 2 -> 6; matrix products, arithmetic and copies ran while one was open for 0% -> 2% of each run, Pallas kernels for 0% -> 0%
where the time goes in v1:
time: 596 us; the launch traced here: 586 us
  waiting for transfers between devices  200 us (34%)
  matrix products  142 us (24%)
  local copies, waits for them, and re-layouts  105 us (18%)
  blocking collectives  96.2 us (16%)
  starting transfers between devices  20.6 us (3%)
  between operations  15.3 us (3%)
  other arithmetic  7.07 us (1%)
    psum x1, waiting for transfers between devices, body(): gram = lax.psum(gram, 'mem')  140 us
    all_gather x1, blocking collectives, body(): lax.all_gather(meta, ('cls', 'mem'), tiled=False)  96.2 us
    ppermute x7, waiting for transfers between devices, pairwise_exchange(): lax.ppermute(sent, axis, [(i, i ^ step) for i in range(size)])  59.4 us
    dot_general x1, matrix products, body(): chosen = jnp.dot(table, proj, preferred_element_type=jnp.float32)  56 us
    unnamed x76, local copies, waits for them, and re-layouts  34.6 us
    dot_general x4, matrix products, tree(): k = jnp.einsum('aibk,blk->aibl', k, c, precision=HI)  34.3 us
    dot_general x4, matrix products, tree(): k = jnp.einsum('aij,ajbk->aibk', c, k, precision=HI)  16.8 us
    reshape x2, local copies, waits for them, and re-layouts, tree(): k = gram.reshape(n_mem, rank, n_mem, rank)  16.5 us
  transfers between devices with their start and end apart: 9, of which 6 were waited for; matrix products, arithmetic and copies ran while one was open for 2% of the time, Pallas kernels for 0%

profile of v1, /device:TPU:1, one launch (start us, length us, event | category | flops | bytes accessed | tf_op | source)
XLA Modules:
  0.0 585.9 jit_solution(7394184300320561026)
XLA Ops:
  6.5 4.0 copy.219
  10.6 8.5 %all-to-all-start = ((bf16[24,16,4096]{2,0,1:T(8,128)(2,1)}), bf16[24,16,4096]{2,0,1:T(8,128)(2,1)}, u32[]{:S(2)}, u32[]{:S(2)}) async-start(bf16[24,16,4096]{2,0,1:T(8,128)(2,1)} %bitcast.306), calls=%async_computation | async-start | bytes 6291456 | tf_op jit(solution)/shard_map/all_to_all | solution.py:101
  19.5 96.2 %all-gather.1 = f32[128,3,24]{2,1,0:T(4,128)S(1)} all-gather(f32[1,3,24]{2,1,0:T(4,128)S(1)} %maximum_bitcast_fusion), channel_id=2, replica_groups=mesh['cls'=8,'mem'=16] {'cls','mem'}, dimensions={0}, use_global_device_ids=true | all-gather | bytes 37152 | tf_op jit(solution)/shard_map/all_gather | solution.py:100
  117.4 3.8 convolution_convert_fusion.1
  121.2 3.4 copy.127
  124.6 3.4 copy.128
  128.1 16.1 %constant_dynamic-slice_fusion = (bf16[1,96,4096]{2,0,1:T(2,128)(2,1)}, bf16[1,96,4096]{2,0,1:T(2,128)(2,1)}, bf16[1,96,4096]{2,0,1:T(2,128)(2,1)}, bf16[1,96,40...) fusion(bf16[8,96,4096]{2,0,1:T(8,128)(2,1)S(1)} %bitcast.301, ...), kind=kLoop, calls=%fused_computation.218 | loop fusion | bytes 12582944 | tf_op jit(solution)/shard_map/dynamic_slice | solution.py:28
  144.2 2.4 copy.220
  146.6 2.4 copy.221
  149.0 2.3 copy.222
  165.9 9.3 %collective-permute-done.1 = bf16[96,4096]{1,0:T(8,128)(2,1)S(1)} collective-permute-done((bf16[96,4096]{1,0:T(8,128)(2,1)S(1)}, bf16[96,4096]{1,0:T(8,128)(2,1)S(1)}, u32[]{:S(2)}, u32[]{:S(2)}) %collective-permute-start.1) | collective-permute-done | bytes 786464 | tf_op jit(solution)/shard_map/ppermute | solution.py:29
  175.2 3.7 collective-permute-start.6
  179.9 13.1 %collective-permute-done.2 = bf16[96,4096]{1,0:T(8,128)(2,1)S(1)} collective-permute-done((bf16[96,4096]{1,0:T(8,128)(2,1)S(1)}, bf16[96,4096]{1,0:T(8,128)(2,1)S(1)}, u32[]{:S(2)}, u32[]{:S(2)}) %collective-permute-start.2) | collective-permute-done | bytes 786464 | tf_op jit(solution)/shard_map/ppermute | solution.py:29
  194.0 16.4 %collective-permute-done.3 = bf16[96,4096]{1,0:T(8,128)(2,1)S(1)} collective-permute-done((bf16[96,4096]{1,0:T(8,128)(2,1)S(1)}, bf16[96,4096]{1,0:T(8,128)(2,1)S(1)}, u32[]{:S(2)}, u32[]{:S(2)}) %collective-permute-start.3) | collective-permute-done | bytes 786464 | tf_op jit(solution)/shard_map/ppermute | solution.py:29
  211.3 16.5 %collective-permute-done.4 = bf16[96,4096]{1,0:T(8,128)(2,1)S(1)} collective-permute-done((bf16[96,4096]{1,0:T(8,128)(2,1)S(1)}, bf16[96,4096]{1,0:T(8,128)(2,1)S(1)}, u32[]{:S(2)}, u32[]{:S(2)}) %collective-permute-start.4) | collective-permute-done | bytes 786464 | tf_op jit(solution)/shard_map/ppermute | solution.py:29
  229.8 4.1 collective-permute-done.6
  234.9 6.4 %gather_fusion = bf16[8,96,4096]{2,1,0:T(8,128)(2,1)} fusion(bf16[8,96,4096]{2,1,0:T(8,128)(2,1)} %bitcast_dynamic-update-slice_fusion, s32[1024]{0:T(1024)S(1)} %pad_clamp_fusion), kind=kCustom, calls=%fused_computation | custom fusion | bytes 12582944 | tf_op jit(solution)/shard_map/gather | solution.py:30
  241.3 56.0 %fusion = bf16[768,4096]{1,0:T(8,128)(2,1)} fusion(bf16[8,96,4096]{2,1,0:T(8,128)(2,1)} %gather_fusion, f32[4096]{0:T(1024)S(1)} %fusion.86, f32[768]{0:T(1024)S(1)} %mul.219, f32[768]{0:T(1024)S(1)} %eq.134, pred[768]{0:T(1024)(128)(4,1)S(1)} %gt.16, bf16[8,65536]{1,0:T(8,128)(2,1)S(1)} %copy-done, s32[]{:T(128)S(6)} %select_n.120), kind=kOutput, calls=%fused_computation.2 | convolution fusion | flops 72376320 | bytes 12674052 | tf_op jit(solution)/shard_map/dot_general | solution.py:123
  297.2 10.1 %reshape.284 = bf16[8,16,6,4096]{3,2,1,0:T(8,128)(2,1)} reshape(bf16[768,4096]{1,0:T(8,128)(2,1)} %fusion) | data formatting | bytes 12582912 | tf_op jit(solution)/shard_map/reshape | solution.py:128
  307.4 7.0 %copy.137 = bf16[16,8,6,4096]{3,0,2,1:T(8,128)(2,1)S(1)} copy(bf16[16,8,6,4096]{3,2,0,1:T(8,128)(2,1)} %bitcast.302) | data formatting | bytes 12582912 | tf_op jit(solution)/shard_map/transpose | solution.py:129
  314.3 5.7 convolution_convert_fusion
  320.0 3.2 copy-done.2
  323.2 10.8 %fusion.142 = f32[1024,1024]{1,0:T(8,128)} fusion(bf16[1024,4096]{1,0:T(8,128)(2,1)S(1)} %bitcast.299), kind=kOutput, calls=%fused_computation.270 | convolution fusion | flops 8589934592 | bytes 12582912 | tf_op jit(solution)/shard_map/ap,bp->ab/dot_general | solution.py:136
  334.0 7.3 %reshape.287 = f32[16,64,16,64]{3,2,1,0:T(8,128)} reshape(f32[1024,1024]{1,0:T(8,128)} %fusion.142) | data formatting | bytes 8388608 | tf_op jit(solution)/shard_map/reshape | solution.py:59
  341.3 9.2 %copy.139 = f32[16,64,16,64]{3,1,2,0:T(8,128)} copy(f32[16,64,16,64]{3,2,1,0:T(8,128)} %reshape.287) | data formatting | bytes 8388608 | tf_op jit(solution)/shard_map/reshape | solution.py:59
  350.6 140.2 %all-reduce.2.cloned.1.call-done = f32[16,64,16,64]{3,1,2,0:T(8,128)} async-done(((f32[16,64,16,64]{3,1,2,0:T(8,128)}), f32[16,64,16,64]{3,1,2,0:T(8,128)}) %all-reduce.2.cloned.1.call-update) | async-done | bytes 4194320 | tf_op jit(solution)/shard_map/psum | solution.py:137
  506.0 8.7 %fusion.1 = f32[16,64,16,64]{3,1,0,2:T(8,128)S(1)} fusion(f32[16,64,16,64]{3,1,2,0:T(8,128)S(1)} %copy-done.3, f32[16,64,64]{2,1,0:T(8,128)S(1)} %convolution_multiply_fusion), kind=kOutput, calls=%fused_computation.3 | convolution fusion | flops 805306368 | bytes 8650752 | tf_op jit(solution)/shard_map/aij,ajbk->aibk/dot_general | solution.py:70
  514.7 26.4 %fusion.16 = f32[16,64,16,64]{3,1,2,0:T(8,128)} fusion(f32[16,64,16,64]{3,1,0,2:T(8,128)S(1)} %fusion.1, f32[16,64,64]{2,1,0:T(8,128)S(1)} %convolution_multiply_fusion), kind=kOutput, calls=%fused_computation.52 | convolution fusion | flops 805306368 | bytes 8650752 | tf_op jit(solution)/shard_map/aibk,blk->aibl/dot_general | solution.py:71
  541.1 4.6 reduce_sum.131
  548.1 6.1 %fusion.28 = f32[8,64,8,64]{3,1,0,2:T(8,128)S(1)} fusion(f32[8,64,8,64]{1,3,0,2:T(8,128)S(1)} %reduce_sum.131, f32[8,64,64]{2,1,0:T(8,128)S(1)} %convolution_multiply_fusion.2), kind=kOutput, calls=%fused_computation.69 | convolution fusion | flops 201326592 | bytes 2228224 | tf_op jit(solution)/shard_map/aij,ajbk->aibk/dot_general | solution.py:70
  555.5 6.0 %fusion.26 = f32[8,64,8,64]{3,1,2,0:T(8,128)S(1)} fusion(f32[8,64,8,64]{3,1,0,2:T(8,128)S(1)} %fusion.28, f32[8,64,64]{2,1,0:T(8,128)S(1)} %convolution_multiply_fusion.2), kind=kOutput, calls=%fused_computation.67 | convolution fusion | flops 201326592 | bytes 2228224 | tf_op jit(solution)/shard_map/aibk,blk->aibl/dot_general | solution.py:71
  572.9 5.7 fusion.4
  (151 shorter events, 51.6 us)
Async XLA Ops:
  6.5 234.7 %copy-start = (bf16[8,65536]{1,0:T(8,128)(2,1)S(1)}, bf16[8,65536]{1,0:T(8,128)(2,1)}, u32[]{:S(2)}) copy-start(bf16[8,65536]{1,0:T(8,128)(2,1)} %param.10) | copy-start | bytes 3145732
  6.5 12.6 %copy-start.10 = (s32[24,1]{0,1:T(1,128)S(1)}, s32[24,1]{0,1:T(1,128)}, u32[]{:S(2)}) copy-start(s32[24,1]{0,1:T(1,128)} %param.7) | copy-start | bytes 292
  6.5 12.9 %copy-start.11 = (s32[24]{0:T(128)S(1)}, s32[24]{0:T(128)}, u32[]{:S(2)}) copy-start(s32[24]{0:T(128)} %param.8) | copy-start | bytes 292
  6.5 12.9 %copy-start.12 = (bf16[24]{0:T(256)(128)(2,1)S(1)}, bf16[24]{0:T(256)(128)(2,1)}, u32[]{:S(2)}) copy-start(bf16[24]{0:T(256)(128)(2,1)} %param.9) | copy-start | bytes 148
  10.6 106.8 %all-to-all-start = ((bf16[24,16,4096]{2,0,1:T(8,128)(2,1)}), bf16[24,16,4096]{2,0,1:T(8,128)(2,1)}, u32[]{:S(2)}, u32[]{:S(2)}) async-start(bf16[24,16,4096]{2,0,1:T(8,128)(2,1)} %bitcast.306), calls=%async_computation | async-start | bytes 6291456 | tf_op jit(solution)/shard_map/all_to_all | solution.py:101
  19.1 471.7 %all-reduce.2.cloned.1.call-start = ((), (), s32[]{:S(2)}) async-start(), calls=%async_computation.1 | async-start | bytes 16777216 | tf_op jit(solution)/shard_map/psum | solution.py:137
  144.2 7.1 %copy-start.7 = (bf16[1,96,4096]{2,0,1:T(2,128)(2,1)S(1)}, bf16[1,96,4096]{2,0,1:T(2,128)(2,1)}, u32[]{:S(2)}) copy-start(bf16[1,96,4096]{2,0,1:T(2,128)(2,1)} %get-tuple-element.11) | copy-start | bytes 2359300
  144.2 8.0 %copy-start.6 = (bf16[1,96,4096]{2,0,1:T(2,128)(2,1)S(1)}, bf16[1,96,4096]{2,0,1:T(2,128)(2,1)}, u32[]{:S(2)}) copy-start(bf16[1,96,4096]{2,0,1:T(2,128)(2,1)} %get-tuple-element.12) | copy-start | bytes 2359300
  144.2 8.9 %copy-start.5 = (bf16[1,96,4096]{2,0,1:T(2,128)(2,1)S(1)}, bf16[1,96,4096]{2,0,1:T(2,128)(2,1)}, u32[]{:S(2)}) copy-start(bf16[1,96,4096]{2,0,1:T(2,128)(2,1)} %get-tuple-element.13) | copy-start | bytes 2359300
  146.6 7.3 %copy-start.4 = (bf16[1,96,4096]{2,0,1:T(2,128)(2,1)S(1)}, bf16[1,96,4096]{2,0,1:T(2,128)(2,1)}, u32[]{:S(2)}) copy-start(bf16[1,96,4096]{2,0,1:T(2,128)(2,1)} %get-tuple-element.14) | copy-start | bytes 2359300
  154.8 8.1 %collective-permute-start = (bf16[96,4096]{1,0:T(8,128)(2,1)S(1)}, bf16[96,4096]{1,0:T(8,128)(2,1)S(1)}, u32[]{:S(2)}, u32[]{:S(2)}) collective-permute-start(bf16[96,4096]{1,0:T(8,128)(2,1)S(1)} %bitcast.323), channel_id=1, source_target_pairs={{0,16},{16,0},{32,48},{48,32},{64,80},{80,64},{96,112},{112,96},{1... | collective-permute-start | bytes 2359304 | tf_op jit(solution)/shard_map/ppermute | solution.py:29
  156.1 19.1 %collective-permute-start.1 = (bf16[96,4096]{1,0:T(8,128)(2,1)S(1)}, bf16[96,4096]{1,0:T(8,128)(2,1)S(1)}, u32[]{:S(2)}, u32[]{:S(2)}) collective-permute-start(bf16[96,4096]{1,0:T(8,128)(2,1)S(1)} %bitcast.322), channel_id=1, source_target_pairs={{0,32},{16,48},{32,0},{48,16},{64,96},{80,112},{96,64},{112,80},{1... | collective-permute-start | bytes 2359304 | tf_op jit(solution)/shard_map/ppermute | solution.py:29
  156.1 36.9 %collective-permute-start.2 = (bf16[96,4096]{1,0:T(8,128)(2,1)S(1)}, bf16[96,4096]{1,0:T(8,128)(2,1)S(1)}, u32[]{:S(2)}, u32[]{:S(2)}) collective-permute-start(bf16[96,4096]{1,0:T(8,128)(2,1)S(1)} %bitcast.321), channel_id=1, source_target_pairs={{0,48},{16,32},{32,16},{48,0},{64,112},{80,96},{96,80},{112,64},{1... | collective-permute-start | bytes 2359304 | tf_op jit(solution)/shard_map/ppermute | solution.py:29
  157.8 52.6 %collective-permute-start.3 = (bf16[96,4096]{1,0:T(8,128)(2,1)S(1)}, bf16[96,4096]{1,0:T(8,128)(2,1)S(1)}, u32[]{:S(2)}, u32[]{:S(2)}) collective-permute-start(bf16[96,4096]{1,0:T(8,128)(2,1)S(1)} %bitcast.320), channel_id=1, source_target_pairs={{0,64},{16,80},{32,96},{48,112},{64,0},{80,16},{96,32},{112,48},{1... | collective-permute-start | bytes 2359304 | tf_op jit(solution)/shard_map/ppermute | solution.py:29
  159.7 68.1 %collective-permute-start.4 = (bf16[96,4096]{1,0:T(8,128)(2,1)S(1)}, bf16[96,4096]{1,0:T(8,128)(2,1)S(1)}, u32[]{:S(2)}, u32[]{:S(2)}) collective-permute-start(bf16[96,4096]{1,0:T(8,128)(2,1)S(1)} %bitcast.319), channel_id=1, source_target_pairs={{0,80},{16,64},{32,112},{48,96},{64,16},{80,0},{96,48},{112,32},{1... | collective-permute-start | bytes 2359304 | tf_op jit(solution)/shard_map/ppermute | solution.py:29
  162.9 66.0 %collective-permute-start.5 = (bf16[96,4096]{1,0:T(8,128)(2,1)S(1)}, bf16[96,4096]{1,0:T(8,128)(2,1)S(1)}, u32[]{:S(2)}, u32[]{:S(2)}) collective-permute-start(bf16[96,4096]{1,0:T(8,128)(2,1)S(1)} %bitcast.318), channel_id=1, source_target_pairs={{0,96},{16,112},{32,64},{48,80},{64,32},{80,48},{96,0},{112,16},{1... | collective-permute-start | bytes 2359304 | tf_op jit(solution)/shard_map/ppermute | solution.py:29
  175.2 58.7 %collective-permute-start.6 = (bf16[96,4096]{1,0:T(8,128)(2,1)S(1)}, bf16[96,4096]{1,0:T(8,128)(2,1)S(1)}, u32[]{:S(2)}, u32[]{:S(2)}) collective-permute-start(bf16[96,4096]{1,0:T(8,128)(2,1)S(1)} %bitcast.317), channel_id=1, source_target_pairs={{0,112},{16,96},{32,80},{48,64},{64,48},{80,32},{96,16},{112,0},{1... | collective-permute-start | bytes 2359304 | tf_op jit(solution)/shard_map/ppermute | solution.py:29
  307.4 7.0 %copy-start.9 = (bf16[64,48]{0,1:T(8,128)(2,1)S(1)}, bf16[64,48]{0,1:T(8,128)(2,1)}, u32[]{:S(2)}) copy-start(bf16[64,48]{0,1:T(8,128)(2,1)} %param.11) | copy-start | bytes 18436
  320.0 3.2 copy-start.2
  490.7 15.3 %copy-start.3 = (f32[16,64,16,64]{3,1,2,0:T(8,128)S(1)}, f32[16,64,16,64]{3,1,2,0:T(8,128)}, u32[]{:S(2)}) copy-start(f32[16,64,16,64]{3,1,2,0:T(8,128)} %all-reduce.2.cloned.1.call-done) | copy-start | bytes 12582916
  561.6 3.4 copy-start.8
  572.5 6.1 %copy-start.1 = (bf16[8,65536]{1,0:T(8,128)(2,1)S(1)}, bf16[8,65536]{1,0:T(8,128)(2,1)}, u32[]{:S(2)}) copy-start(bf16[8,65536]{1,0:T(8,128)(2,1)} %param.10) | copy-start | bytes 3145732
Sparse Core Ops, SparseCore 0:
  350.7 140.0 all-reduce.1
